TPU v7x, 256 devices: a whole 4x4x8 slice. The times are simulated.
256 devices in a mesh: chan: 16 (over x, y), tm: 16 (over z, core).
Axes of the slice: x: 4, y: 4, z: 8, core: 2. Of those that a mesh axis runs over, the one named last changes fastest.
Arguments:
- records: bfloat16 [16, 6144, 1536], P('tm', 'chan')
- partners: int32 [16, 3], P('chan'), may hold values from 0 to 15, as said below
- counts: int32 [16], P('chan'), may hold values from 1 to 3, as said below
- sources: int32 [16, 2], P('chan'), may hold values from 0 to 383, as said below
Outputs:
- xcorr: float32 [16, 384, 3, 2, 384], P('chan', 'tm')
Inputs may be any that keep to these rules, and one draw needn't show every extreme that they name: `partners`: each row holds 3 different blocks. `counts`: some block has all 3 slots live. `sources`: each row holds 2 different channels.
All inputs are finite; a program needn't handle non-finite values.
Results may differ from a plain program's by a relative error of at most 0.008.
Values may be sent and summed in bfloat16 or wider, within the bound.
A program may use at most 64 MiB of HBM per device.

v0:
```python
import math

import jax
import jax.numpy as jnp
from jax import lax
from jax.sharding import PartitionSpec as P

L = 1536
F = 320
HL = 192
SMOOTH = 32


def dft_table(length, bins):
    sample_index = jnp.arange(length, dtype=jnp.int32)[:, None]
    bin_index = jnp.arange(bins, dtype=jnp.int32)[None, :] + 1
    phase_index = sample_index * bin_index % length
    angle = phase_index.astype(jnp.float32) * (2.0 * math.pi / length)
    return jnp.concatenate([jnp.cos(angle), -jnp.sin(angle)], axis=1).astype(jnp.bfloat16)


def lag_table(length, bins, half):
    bin_index = jnp.arange(bins, dtype=jnp.int32)[:, None] + 1
    lag_index = jnp.arange(2 * half, dtype=jnp.int32)[None, :] - half
    phase_index = jnp.mod(bin_index * lag_index, length)
    angle = phase_index.astype(jnp.float32) * (2.0 * math.pi / length)
    return jnp.concatenate([jnp.cos(angle), -jnp.sin(angle)], axis=0)


def band_table(bins, half):
    input_bin = jnp.arange(bins, dtype=jnp.int32)[:, None]
    output_bin = jnp.arange(bins, dtype=jnp.int32)[None, :]
    centre = jnp.clip(output_bin, half, bins - 1 - half)
    return (jnp.abs(input_bin - centre) <= half).astype(jnp.float32)


def whiten(block_records):
    windows, channels, length = block_records.shape
    signal = block_records.astype(jnp.float32)
    signal = signal - jnp.mean(signal, axis=-1, keepdims=True)
    demeaned = signal.astype(jnp.bfloat16).reshape(windows * channels, length)
    spectrum = jnp.dot(demeaned, dft_table(L, F), preferred_element_type=jnp.float32)
    real_part = spectrum[:, :F]
    imag_part = spectrum[:, F:]
    amplitude = jnp.sqrt(real_part * real_part + imag_part * imag_part)
    smooth = jnp.dot(amplitude, band_table(F, SMOOTH), precision=lax.Precision.HIGHEST) / (
        2 * SMOOTH + 1
    )
    factor = 1.0 / (smooth + 1e-06)
    whitened = jnp.concatenate([real_part * factor, imag_part * factor], axis=1)
    return whitened.astype(jnp.bfloat16).reshape(windows, channels, 2 * F)


def cross_terms(source_spec, partner_white):
    src_real = source_spec[..., :F]
    src_imag = source_spec[..., F:]
    rec_real = partner_white[..., :F]
    rec_imag = partner_white[..., F:]
    cross_real = jnp.einsum(
        "wsf,pwcf->cpsf", src_real, rec_real, preferred_element_type=jnp.float32
    ) + jnp.einsum("wsf,pwcf->cpsf", src_imag, rec_imag, preferred_element_type=jnp.float32)
    cross_imag = jnp.einsum(
        "wsf,pwcf->cpsf", src_real, rec_imag, preferred_element_type=jnp.float32
    ) - jnp.einsum("wsf,pwcf->cpsf", src_imag, rec_real, preferred_element_type=jnp.float32)
    return jnp.concatenate([cross_real, cross_imag], axis=-1)


def local(records, partners, counts, sources):
    windows, channels, length = records.shape
    slots = partners.shape[1]
    white = whiten(records)
    partner_ids = partners[0]
    live = jnp.arange(slots, dtype=jnp.int32) < counts[0]
    piece = lax.all_gather(white, "chan", axis=1, tiled=True)
    blocks_here = piece.shape[1] // channels
    block_ids = jnp.arange(blocks_here, dtype=jnp.int32)
    matches = ((block_ids[None, :] == partner_ids[:, None]) & live[:, None]).astype(jnp.bfloat16)
    shaped = piece.reshape(windows, blocks_here, channels, piece.shape[2])
    partner_white = jnp.einsum(
        "pj,wjcf->pwcf", matches, shaped, preferred_element_type=jnp.float32
    ).astype(jnp.bfloat16)
    picker = (jnp.arange(channels, dtype=jnp.int32)[None, :] == sources[0][:, None]).astype(
        jnp.bfloat16
    )
    source_spec = jnp.einsum(
        "sc,wcf->wsf", picker, white, preferred_element_type=jnp.float32
    ).astype(jnp.bfloat16)
    sources_count = source_spec.shape[1]
    inverse = lag_table(L, F, HL)
    scale = 1.0 / math.sqrt(F * windows * lax.axis_size("tm"))
    share_rows = channels // lax.axis_size("tm")
    stacked = cross_terms(source_spec, partner_white)
    summed = lax.psum_scatter(stacked, "tm", scatter_dimension=0, tiled=True)
    lagged = jnp.dot(
        summed.reshape(share_rows * slots * sources_count, 2 * F),
        inverse,
        precision=lax.Precision.HIGHEST,
    )
    result = lagged.reshape(share_rows, slots, sources_count, 2 * HL) * scale
    return result[None]


def solution(mesh):
    return jax.shard_map(
        local,
        mesh=mesh,
        in_specs=(P("tm", "chan", None), P("chan", None), P("chan"), P("chan", None)),
        out_specs=P("chan", "tm", None, None, None),
        check_vma=False,
    )
```

profile of v0, /device:TPU:1, one launch (start us, length us, event | category | flops | bytes accessed | tf_op | source)
XLA Modules:
  0.0 184.0 jit_solution(6916343911090276861)
XLA Ops:
  6.5 0.0 copy-start
  6.5 0.0 all-gather.2.cloned.1.call-start
  6.5 10.0 %cosine_convert_fusion = (bf16[1536,320]{1,0:T(8,128)(2,1)S(1)}, bf16[1536,320]{1,0:T(8,128)(2,1)S(1)}) fusion(s32[320]{0:T(512)S(1)} %iota_add_fusion.1), kind=kLoop, calls=%fused_computation.14 | loop fusion | flops 5898240 | bytes 1967360 | tf_op jit(solution)/shard_map/convert.30
  16.6 0.0 copy-done
  16.6 0.2 convert_reduce_fusion
  16.8 1.2 fusion.8
  18.0 0.0 copy-start.2
  18.0 0.0 copy-start.1
  18.0 1.1 multiply_convert_fusion.1
  19.1 1.0 pad_maximum_fusion.1
  20.0 0.0 all-gather.2.cloned.1.call-update
  20.1 0.2 reduce-scatter.2.cloned.1.call-start
  21.0 0.0 copy-done.2
  21.0 0.3 fusion.20
  21.2 0.1 convert_bitcast_fusion.4
  21.3 76.0 %all-gather.2.cloned.1.call-done = bf16[1,6144,640]{2,1,0:T(8,128)(2,1)} async-done(((bf16[1,384,640]{2,1,0:T(8,128)(2,1)}), bf16[1,6144,640]{2,1,0:T(8,128)(2,1)}) %all-gather.2.cloned.1.call-update) | async-done | bytes 7864336 | tf_op jit(solution)/shard_map/all_gather | solution.py:74
  97.4 0.0 copy-done.1
  97.4 7.9 %convert_bitcast_fusion.2 = bf16[3,1,384,640]{3,0,2,1:T(4,128)(2,1)S(1)} fusion(bf16[16,384,640]{2,1,0:T(8,128)(2,1)} %bitcast.59, s32[3]{0:T(128)S(1)} %bitcast.62, pred[3]{0:T(512)(128)(4,1)S(1)} %iota_compare_fusion.1), kind=kOutput, calls=%fused_computation.23 | convolution fusion | flops 24330336 | bytes 9338895 | tf_op jit(solution)/shard_map/pj,wjcf->pwcf/dot_general | solution.py:79
  105.3 1.2 convert_bitcast_fusion.1
  106.4 0.1 copy.7
  106.6 0.1 copy.8
  106.7 0.9 add_bitcast_fusion
  107.6 3.6 %pad_maximum_fusion = f32[384,3,2,640]{3,0,2,1:T(8,128)} fusion(f32[384,3,2,320]{3,0,2,1:T(8,128)S(1)} %get-tuple-element.6, f32[384,3,2,320]{3,0,2,1:T(8,128)S(1)} %get-tuple-element.5), kind=kLoop, calls=%fused_computation.2 | loop fusion | flops 1474560 | bytes 11796480 | tf_op jit(solution)/shard_map/concatenate | solution.py:65
  111.2 0.0 reduce-scatter.2.cloned.1.call-update
  111.2 2.1 %fusion.36 = (f32[320,384]{1,0:T(8,128)S(1)}, f32[320,384]{1,0:T(8,128)S(1)}) fusion(s32[384]{0:T(512)S(1)} %iota_add_fusion, s32[320]{0:T(512)S(1)} %iota_add_fusion.1), kind=kLoop, calls=%fused_computation.57 | loop fusion | flops 1228800 | bytes 985856 | tf_op jit(solution)/shard_map/cos | solution.py:27
  113.3 61.2 %reduce-scatter.2.cloned.1.call-done = f32[24,3,2,640]{3,0,2,1:T(8,128)} async-done(((f32[384,3,2,640]{3,0,2,1:T(8,128)}), f32[24,3,2,640]{3,0,2,1:T(8,128)}) %reduce-scatter.2.cloned.1.call-update) | async-done | bytes 368656 | tf_op jit(solution)/shard_map/reduce_scatter | solution.py:93
  174.5 1.9 %fusion.19 = f32[1,24,3,2,384]{4,1,3,2,0:T(8,128)S(1)} fusion(f32[24,3,2,640]{3,0,2,1:T(8,128)} %reduce-scatter.2.cloned.1.call-done, f32[320,384]{1,0:T(8,128)S(1)} %get-tuple-element.12, f32[320,384]{1,0:T(8,128)S(1)} %get-tuple-element.11), kind=kOutput, calls=%fused_computation.32 | convolution fusion | flops 424974336 | bytes 1572864 | tf_op jit(solution)/shard_map/dot_general | solution.py:94
  176.4 0.8 copy.9
  (5 shorter events, 0.0 us)
Async XLA Ops:
  6.5 10.0 %copy-start = (bf16[1,384,1536]{2,1,0:T(8,128)(2,1)S(1)}, bf16[1,384,1536]{2,1,0:T(8,128)(2,1)}, u32[]{:S(2)}) copy-start(bf16[1,384,1536]{2,1,0:T(8,128)(2,1)} %param.4) | copy-start | bytes 3538948
  6.5 90.8 %all-gather.2.cloned.1.call-start = ((), (), s32[]{:S(2)}) async-start(), calls=%async_computation.1 | async-start | bytes 8355840 | tf_op jit(solution)/shard_map/all_gather | solution.py:74
  18.0 3.0 %copy-start.2 = (s32[1,2]{1,0:T(1,128)S(1)}, s32[1,2]{1,0:T(1,128)}, u32[]{:S(2)}) copy-start(s32[1,2]{1,0:T(1,128)} %param.7) | copy-start | bytes 28
  18.0 79.4 %copy-start.1 = (s32[1,3]{1,0:T(1,128)S(1)}, s32[1,3]{1,0:T(1,128)}, u32[]{:S(2)}) copy-start(s32[1,3]{1,0:T(1,128)} %param.5) | copy-start | bytes 40
  20.1 154.4 %reduce-scatter.2.cloned.1.call-start = ((), (), s32[]{:S(2)}) async-start(), calls=%async_computation.2 | async-start | bytes 6266880 | tf_op jit(solution)/shard_map/reduce_scatter | solution.py:93
Sparse Core Ops, SparseCore 0:
  20.2 77.1 all-gather.1
  111.4 63.0 reduce-scatter.1
where the time goes:
time: 187 us; the launch traced here: 184 us
  waiting for transfers between devices  137 us (73%)
  other arithmetic  19.1 us (10%)
  between operations  14.2 us (8%)
  matrix products  12.3 us (7%)
    all_gather x1, waiting for transfers between devices, local(): piece = lax.all_gather(white, 'chan', axis=1, tiled=True)  76 us
    reduce_scatter x1, waiting for transfers between devices, local(): summed = lax.psum_scatter(stacked, 'tm', scatter_dimension=0, tiled=True)  61.2 us
    another operation x3, other arithmetic  11.2 us
    dot_general x1, matrix products, local(): jnp.einsum('pj,wjcf->pwcf', matches, shaped, preferred_element_type=jnp.f...  7.9 us
  transfers between devices with their start and end apart: 2, of which 2 were waited for; matrix products, arithmetic and copies ran while one was open for 1% of the time, Pallas kernels for 0%

commit v1 on v0

v1 whole, which is shorter than its diff:
```python
import functools
import math

import jax
import jax.numpy as jnp
import ml_dtypes
import numpy as np
from jax import lax
from jax.experimental import pallas as pl
from jax.experimental.pallas import tpu as pltpu
from jax.sharding import PartitionSpec as P

L = 1536
F = 320
HL = 192
SMOOTH = 32
ROWS = 8
LANES = 128
FULL = 256
HALF = F - FULL
COLS = 2 * F
MESH = pl.DeviceIdType.MESH


def tables():
    sample_index = np.arange(L, dtype=np.int64)[:, None]
    bin_index = np.arange(F, dtype=np.int64)[None, :] + 1
    phase_index = sample_index * bin_index % L
    angle = phase_index.astype(np.float32) * np.float32(2.0 * math.pi / L)
    cosine, sine = np.cos(angle), -np.sin(angle)
    table = np.concatenate(
        [cosine[:, :FULL], sine[:, :FULL], cosine[:, FULL:], sine[:, FULL:]], axis=1
    ).astype(np.float32)
    high = table.astype(ml_dtypes.bfloat16)
    lag_rows = np.concatenate([np.arange(L - HL, L), np.arange(HL)])
    low = (table - high.astype(np.float32)).astype(ml_dtypes.bfloat16)[lag_rows]
    return high, low


def dot(left, right):
    return jnp.dot(left, right, preferred_element_type=jnp.float32)


def dot_rows(left, right):
    return lax.dot_general(left, right, (((1,), (1,)), ((), ())), preferred_element_type=jnp.float32)


def split(value):
    high = value.astype(jnp.bfloat16)
    return high, (value - high.astype(jnp.float32)).astype(jnp.bfloat16)


def band_matrix():
    width = FULL + LANES
    row = lax.broadcasted_iota(jnp.int32, (width, width), 0)
    col = lax.broadcasted_iota(jnp.int32, (width, width), 1)
    out_bin = jnp.where(col < F, col, col - HALF)
    centre = jnp.clip(out_bin, SMOOTH, F - 1 - SMOOTH)
    near = (jnp.abs(row - centre) <= SMOOTH) & (row < F)
    return jnp.where(near, 1.0, 0.0).astype(jnp.bfloat16)


def whiten(signal, table, band):
    mean = jnp.sum(signal, axis=1, keepdims=True) * (1.0 / L)
    spectrum = dot((signal - mean).astype(jnp.bfloat16), table)
    real, imag, mixed = spectrum[:, :FULL], spectrum[:, FULL : 2 * FULL], spectrum[:, 2 * FULL :]
    squares = mixed * mixed
    power = jnp.concatenate([real * real + imag * imag, squares + pltpu.roll(squares, HALF, 1)], axis=1)
    amplitude = jnp.sqrt(power)
    first, rest = split(amplitude)
    second, third = split(amplitude - first.astype(jnp.float32))
    smooth = (dot(first, band) + dot(second, band) + dot(third, band)) / (2 * SMOOTH + 1)
    factor = 1.0 / (smooth + 1e-06)
    return jnp.concatenate(
        [real * factor[:, :FULL], imag * factor[:, :FULL], mixed * factor[:, FULL:]], axis=1
    )


def kernel(
    dims,
    rec_hbm,
    table_hbm,
    low_hbm,
    partners_ref,
    counts_ref,
    sources_ref,
    out_ref,
    rec,
    table,
    lag_high,
    lag_low,
    band,
    white_send,
    white_recv,
    near_send,
    near_recv,
    near_rows,
    far_send,
    far_recv,
    source_rows,
    partner_rows,
    cross,
    stack_send,
    stack_recvs,
    local_sems,
    near_sems,
    far_sems,
    white_sems,
    stack_sems,
):
    blocks, shares, pieces, slots, sources = dims
    me_chan, me_tm = lax.axis_index("chan"), lax.axis_index("tm")

    def others(axis, me, size):
        return [(axis, lax.rem(me + step, size)) for step in range(1, size)]

    tm_peers = others("tm", me_tm, shares)
    chan_peers = others("chan", me_chan, blocks)

    barrier = pltpu.get_barrier_semaphore()
    for axis, peer in tm_peers + chan_peers:
        pl.semaphore_signal(barrier, inc=1, device_id={axis: peer}, device_id_type=MESH)

    loads = [pltpu.make_async_copy(rec_hbm.at[:, piece], rec.at[piece], local_sems.at[piece]) for piece in range(pieces)]
    table_load = pltpu.make_async_copy(table_hbm, table, local_sems.at[pieces])
    lag_loads = [
        pltpu.make_async_copy(table_hbm.at[pl.ds(L - HL, HL)], lag_high.at[pl.ds(0, HL)], local_sems.at[pieces + 1]),
        pltpu.make_async_copy(table_hbm.at[pl.ds(0, HL)], lag_high.at[pl.ds(HL, HL)], local_sems.at[pieces + 2]),
        pltpu.make_async_copy(low_hbm, lag_low, local_sems.at[pieces + 3]),
    ]
    for copy in loads + [table_load] + lag_loads:
        copy.start()

    def send(src, dst, sems, peer):
        axis, index = peer
        pltpu.make_async_remote_copy(
            src_ref=src, dst_ref=dst, send_sem=sems[0], recv_sem=sems[1], device_id={axis: index}, device_id_type=MESH
        ).start()

    def wait_bytes(ref, sem):
        pltpu.make_async_copy(ref, ref, sem).wait()

    band[...] = band_matrix()
    for copy in loads:
        copy.wait()

    row_id = lax.broadcasted_iota(jnp.int32, (ROWS, L), 0)
    picked = []
    for source in range(sources):
        channel = sources_ref[source]
        share = lax.div(channel, pieces * ROWS)
        within = channel - share * (pieces * ROWS)
        piece = lax.div(within, ROWS)
        tile = rec[piece, share].astype(jnp.float32)
        picked.append(jnp.sum(jnp.where(row_id == within - piece * ROWS, tile, 0.0), axis=0, keepdims=True))
    head_id = lax.broadcasted_iota(jnp.int32, (2 * ROWS, L), 0)
    head = jnp.broadcast_to(picked[0], (2 * ROWS, L))
    for source in range(1, sources):
        head = jnp.where(head_id == source, picked[source], head)

    table_load.wait()
    for piece in range(pieces):
        signal = rec[piece].astype(jnp.float32).reshape(shares * ROWS, L)
        if piece == 0:
            signal = jnp.concatenate([head, signal], axis=0)
        white = whiten(signal, table[...], band[...])
        if piece == 0:
            near_send[...] = white[:sources].astype(jnp.bfloat16).astype(jnp.float32)
            near_recv[me_tm] = near_send[...]
            white = white[2 * ROWS :]
        white = white.reshape(shares, ROWS, COLS).astype(jnp.bfloat16)
        white_send[piece] = white
        white_recv[piece, me_tm] = white_send[piece, me_tm]
        if piece == 0:
            pl.semaphore_wait(barrier, len(tm_peers) + len(chan_peers))
            for peer in tm_peers:
                send(near_send, near_recv.at[me_tm], (near_sems.at[0], near_sems.at[1]), peer)
        for peer in tm_peers:
            send(
                white_send.at[piece, peer[1]],
                white_recv.at[piece, me_tm],
                (white_sems.at[0, piece], white_sems.at[1, piece]),
                peer,
            )

    wait_bytes(near_recv.at[pl.ds(0, shares - 1)], near_sems.at[1])
    for window in range(shares):
        near_rows[pl.ds(window * sources, sources), :] = near_recv[window]
    far_send[...] = near_rows[...].astype(jnp.bfloat16)
    far_recv[me_chan] = far_send[...]
    for peer in chan_peers:
        send(far_send, far_recv.at[me_chan], (far_sems.at[0], far_sems.at[1]), peer)
    wait_bytes(far_recv.at[pl.ds(0, blocks - 1)], far_sems.at[1])
    for tile in range(COLS // LANES):
        source_rows[:, tile] = far_recv[:, :, pl.ds(tile * LANES, LANES)].astype(jnp.float32)

    for copy in lag_loads:
        copy.wait()
    lane = lax.broadcasted_iota(jnp.int32, (ROWS, LANES), 1)
    scale = 1.0 / math.sqrt(F * shares)

    for piece in range(pieces):
        wait_bytes(white_recv.at[piece, pl.ds(0, shares - 1)], white_sems.at[1, piece])
        spectra = white_recv[piece].astype(jnp.float32)
        partner_rows[:, :, :COLS] = spectra
        partner_rows[:, :, COLS:] = pltpu.roll(spectra[:, :, 2 * FULL :], HALF, 2)

        def per_block(block, carry):
            def source_tile(window, source, tile):
                return source_rows[block, tile, pl.ds(window * sources + source, ROWS, stride=0), :]

            def partner_tile(window, tile):
                return partner_rows[window, :, pl.ds(tile * LANES, LANES)]

            tiles = FULL // LANES
            for tile in range(tiles):
                real, imag = [0.0] * sources, [0.0] * sources
                for window in range(shares):
                    b_re, b_im = partner_tile(window, tile), partner_tile(window, tiles + tile)
                    for source in range(sources):
                        a_re = source_tile(window, source, tile)
                        a_im = source_tile(window, source, tiles + tile)
                        real[source] = real[source] + (a_re * b_re + a_im * b_im)
                        imag[source] = imag[source] + (a_re * b_im - a_im * b_re)
                for source in range(sources):
                    cross[block * sources + source, :, pl.ds(tile * LANES, LANES)] = real[source]
                    cross[block * sources + source, :, pl.ds((tiles + tile) * LANES, LANES)] = imag[source]
            same, other = [0.0] * sources, [0.0] * sources
            for window in range(shares):
                b_mix, b_swap = partner_tile(window, 2 * tiles), partner_tile(window, 2 * tiles + 1)
                for source in range(sources):
                    a_mix = source_tile(window, source, 2 * tiles)
                    same[source] = same[source] + a_mix * b_mix
                    other[source] = other[source] + a_mix * b_swap
            for source in range(sources):
                real_part = same[source] + pltpu.roll(same[source], HALF, 1)
                imag_part = pltpu.roll(other[source], HALF, 1) - other[source]
                cross[block * sources + source, :, pl.ds(2 * FULL, LANES)] = jnp.where(
                    lane < HALF, real_part, imag_part
                )
            return carry

        lax.fori_loop(0, blocks, per_block, 0)
        high, low = split(cross[...].reshape(blocks * sources * ROWS, COLS))
        lagged = dot_rows(high, lag_high[...]) + dot_rows(low, lag_high[...]) + dot_rows(high, lag_low[...])
        stack_send[piece] = (lagged * scale).reshape(blocks, sources, ROWS, 2 * HL).astype(jnp.bfloat16)
        stack_recvs[piece][me_chan] = stack_send[piece, me_chan]
        for peer in chan_peers:
            send(
                stack_send.at[piece, peer[1]],
                stack_recvs[piece].at[me_chan],
                (stack_sems.at[0, piece], stack_sems.at[1, piece]),
                peer,
            )

    for piece in range(pieces):
        wait_bytes(stack_recvs[piece].at[pl.ds(0, blocks - 1)], stack_sems.at[1, piece])
        for slot in range(slots):
            stack = stack_recvs[piece][partners_ref[slot]].astype(jnp.float32)
            out_ref[slot, :, pl.ds(piece * ROWS, ROWS), :] = jnp.where(slot < counts_ref[0], stack, 0.0)

    wait_bytes(near_recv.at[pl.ds(0, shares - 1)], near_sems.at[0])
    wait_bytes(far_recv.at[pl.ds(0, blocks - 1)], far_sems.at[0])
    for piece in range(pieces):
        wait_bytes(white_recv.at[piece, pl.ds(0, shares - 1)], white_sems.at[0, piece])
        wait_bytes(stack_recvs[piece].at[pl.ds(0, blocks - 1)], stack_sems.at[0, piece])


def local(blocks, shares, records, partners, counts, sources):
    channels = records.shape[1]
    slots, picks = partners.shape[1], sources.shape[1]
    pieces = channels // (shares * ROWS)
    high, low = tables()
    any_spec = pl.BlockSpec(memory_space=pl.ANY)
    smem_spec = pl.BlockSpec(memory_space=pltpu.SMEM)
    bf16, f32 = jnp.bfloat16, jnp.float32
    result = pl.pallas_call(
        functools.partial(kernel, (blocks, shares, pieces, slots, picks)),
        out_shape=jax.ShapeDtypeStruct((slots, picks, pieces * ROWS, 2 * HL), f32),
        in_specs=[any_spec] * 3 + [smem_spec] * 3,
        out_specs=pl.BlockSpec(memory_space=pltpu.VMEM),
        scratch_shapes=[
            pltpu.VMEM((pieces, shares, ROWS, L), bf16),
            pltpu.VMEM((L, COLS), bf16),
            pltpu.VMEM((2 * HL, COLS), bf16),
            pltpu.VMEM((2 * HL, COLS), bf16),
            pltpu.VMEM((FULL + LANES, FULL + LANES), bf16),
            pltpu.VMEM((pieces, shares, ROWS, COLS), bf16),
            pltpu.VMEM((pieces, shares, ROWS, COLS), bf16),
            pltpu.VMEM((picks, COLS), f32),
            pltpu.VMEM((shares, picks, COLS), f32),
            pltpu.VMEM((shares * picks, COLS), f32),
            pltpu.VMEM((shares * picks, COLS), bf16),
            pltpu.VMEM((blocks, shares * picks, COLS), bf16),
            pltpu.VMEM((blocks, COLS // LANES, shares * picks, LANES), f32),
            pltpu.VMEM((shares, ROWS, COLS + LANES), f32),
            pltpu.VMEM((blocks * picks, ROWS, COLS), f32),
            pltpu.VMEM((pieces, blocks, picks, ROWS, 2 * HL), bf16),
            [pltpu.VMEM((blocks, picks, ROWS, 2 * HL), bf16) for _ in range(pieces)],
            pltpu.SemaphoreType.DMA((pieces + 4,)),
            pltpu.SemaphoreType.DMA((2,)),
            pltpu.SemaphoreType.DMA((2,)),
            pltpu.SemaphoreType.DMA((2, pieces)),
            pltpu.SemaphoreType.DMA((2, pieces)),
        ],
        compiler_params=pltpu.CompilerParams(
            collective_id=0, has_side_effects=True, vmem_limit_bytes=48 * 1024 * 1024
        ),
        name="correlate",
    )(
        records.reshape(shares, pieces, ROWS, L),
        jnp.asarray(high),
        jnp.asarray(low),
        partners.reshape(slots),
        counts,
        sources.reshape(picks),
    )
    return result.transpose(2, 0, 1, 3)[None]


def solution(mesh):
    return jax.shard_map(
        functools.partial(local, mesh.shape["chan"], mesh.shape["tm"]),
        mesh=mesh,
        in_specs=(P("tm", "chan", None), P("chan", None), P("chan"), P("chan", None)),
        out_specs=P("chan", "tm", None, None, None),
        check_vma=False,
    )
```

time: 187 us -> 48.3 us (0.26); the launches traced: 184 us -> 48 us
  waiting for transfers between devices: 137 us -> 0 us
  Pallas kernels: 0 us -> 41.3 us
  other arithmetic: 19.1 us -> 0 us
  between operations: 14.2 us -> 0.67 us
  matrix products: 12.3 us -> 0 us
  local copies, waits for them, and re-layouts: 1.05 us -> 5.95 us
    all_gather x1 -> x0, waiting for transfers between devices: 76 us -> none  [local(): piece = lax.all_gather(white, 'chan', axis=1, tiled=True)]
    reduce_scatter x1 -> x0, waiting for transfers between devices: 61.2 us -> none  [local(): summed = lax.psum_scatter(stacked, 'tm', scatter_dimension=0, tiled=True)]
    pallas_call x0 -> x1, Pallas kernels: none -> 41.3 us  [local(): pl.pallas_call(functools.partial(kernel, (blocks, shares, pieces, slots,...]
    dot_general x5 -> x0, matrix products: 12.3 us -> none  [the longest x1 7.9 us: local(): jnp.einsum('pj,wjcf->pwcf', matches, shaped, preferred_element_type=jnp.f...]
    another operation x3 -> x0, other arithmetic: 11.2 us -> none
    unnamed x6 -> x10, local copies, waits for them, and re-layouts: 0.02 us -> 5.15 us
    concatenate x2 -> x0, other arithmetic: 4.6 us -> none  [the longest x1 3.62 us: cross_terms(): return jnp.concatenate([cross_real, cross_imag], axis=-1)]
    cos x1 -> x0, other arithmetic: 2.07 us -> none  [lag_table(): return jnp.concatenate([jnp.cos(angle), -jnp.sin(angle)], axis=0)]
  transfers between devices with their start and end apart: 2 -> 0, of which waited for: 2 -> 0; matrix products, arithmetic and copies ran while one was open for 1% -> 0% of each run, Pallas kernels for 0% -> 0%
where the time goes in v1:
time: 48.3 us; the launch traced here: 48 us
  Pallas kernels  41.3 us (86%)
  local copies, waits for them, and re-layouts  5.95 us (12%)
  between operations  0.67 us (1%)
    pallas_call x1, Pallas kernels, local(): pl.pallas_call(functools.partial(kernel, (blocks, shares, pieces, slots,...  41.3 us
    unnamed x10, local copies, waits for them, and re-layouts  5.15 us

profile of v1, /device:TPU:1, one launch (start us, length us, event | category | flops | bytes accessed | tf_op | source)
XLA Modules:
  0.0 48.0 jit_solution(17451405620224209965)
XLA Ops:
  0.7 0.0 copy-start
  0.7 1.5 %copy-done = bf16[1536,640]{1,0:T(8,128)(2,1)S(1)} copy-done((bf16[1536,640]{1,0:T(8,128)(2,1)S(1)}, bf16[1536,640]{1,0:T(8,128)(2,1)}, u32[]{:S(2)}) %copy-start) | copy-done | bytes 1966104
  2.2 0.0 copy-start.1
  2.2 1.3 %copy-done.1 = bf16[1,384,1536]{2,1,0:T(8,128)(2,1)S(1)} copy-done((bf16[1,384,1536]{2,1,0:T(8,128)(2,1)S(1)}, bf16[1,384,1536]{2,1,0:T(8,128)(2,1)}, u32[]{:S(2)}) %copy-start.1) | copy-done | bytes 1179672
  3.5 0.0 copy-start.2
  3.5 1.0 %copy-done.2 = bf16[384,640]{1,0:T(8,128)(2,1)S(1)} copy-done((bf16[384,640]{1,0:T(8,128)(2,1)S(1)}, bf16[384,640]{1,0:T(8,128)(2,1)}, u32[]{:S(2)}) %copy-start.2) | copy-done | bytes 491544
  4.5 0.0 copy-start.3
  4.5 0.7 %copy-done.3 = s32[1,3]{1,0:T(1,128)S(1)} copy-done((s32[1,3]{1,0:T(1,128)S(1)}, s32[1,3]{1,0:T(1,128)}, u32[]{:S(2)}) %copy-start.3) | copy-done | bytes 36
  5.2 0.0 copy-start.4
  5.2 0.7 %copy-done.4 = s32[1,2]{1,0:T(1,128)S(1)} copy-done((s32[1,2]{1,0:T(1,128)S(1)}, s32[1,2]{1,0:T(1,128)}, u32[]{:S(2)}) %copy-start.4) | copy-done | bytes 32
  5.8 41.3 %correlate.1 = f32[3,2,24,384]{3,2,1,0:T(8,128)S(1)} custom-call(bf16[16,3,8,1536]{3,2,1,0:T(8,128)(2,1)S(1)} %bitcast.6, bf16[1536,640]{1,0:T(8,128)(2,1)S(1)} %copy-done, bf16[384,640]{1,0:T(8,128)(2,1)S(1)} %copy-done.2, s32[3]{0:T(128)S(1)} %bitcast.8, s32[1]{0:T(128)S(6)} %copy.8.counts_ref, s32[2]{0:T(128)S(1)} %bitcast.9), custom_call_target="tpu_custom_call" | custom-call | tf_op jit(solution)/shard_map/correlate/pallas_call | solution.py:277
  47.1 0.8 %copy.7 = f32[1,24,3,2,384]{4,3,2,1,0:T(2,128)} copy(f32[1,24,3,2,384]{4,1,3,2,0:T(8,128)S(1)} %bitcast.7) | data formatting | bytes 442368 | tf_op jit(solution)/shard_map/broadcast_in_dim | solution.py:318
Async XLA Ops:
  0.7 1.5 %copy-start = (bf16[1536,640]{1,0:T(8,128)(2,1)S(1)}, bf16[1536,640]{1,0:T(8,128)(2,1)}, u32[]{:S(2)}) copy-start(bf16[1536,640]{1,0:T(8,128)(2,1)} %constant.4.clone.table_hbm) | copy-start | bytes 5898244
  2.2 1.3 %copy-start.1 = (bf16[1,384,1536]{2,1,0:T(8,128)(2,1)S(1)}, bf16[1,384,1536]{2,1,0:T(8,128)(2,1)}, u32[]{:S(2)}) copy-start(bf16[1,384,1536]{2,1,0:T(8,128)(2,1)} %param.6) | copy-start | bytes 3538948
  3.5 1.0 %copy-start.2 = (bf16[384,640]{1,0:T(8,128)(2,1)S(1)}, bf16[384,640]{1,0:T(8,128)(2,1)}, u32[]{:S(2)}) copy-start(bf16[384,640]{1,0:T(8,128)(2,1)} %constant.5.clone.low_hbm) | copy-start | bytes 1474564
  4.5 0.7 %copy-start.3 = (s32[1,3]{1,0:T(1,128)S(1)}, s32[1,3]{1,0:T(1,128)}, u32[]{:S(2)}) copy-start(s32[1,3]{1,0:T(1,128)} %param.7) | copy-start | bytes 40
  5.2 0.7 %copy-start.4 = (s32[1,2]{1,0:T(1,128)S(1)}, s32[1,2]{1,0:T(1,128)}, u32[]{:S(2)}) copy-start(s32[1,2]{1,0:T(1,128)} %param.9) | copy-start | bytes 28

commit v2 on v1

v2 whole, which is shorter than its diff:
```python
import functools
import math

import jax
import jax.numpy as jnp
import ml_dtypes
import numpy as np
from jax import lax
from jax.experimental import pallas as pl
from jax.experimental.pallas import tpu as pltpu
from jax.sharding import PartitionSpec as P

L = 1536
F = 320
HL = 192
SMOOTH = 32
ROWS = 8
LANES = 128
FULL = 256
HALF = F - FULL
COLS = 2 * F
CORES = 2
TOGETHER = 2
MESH = pl.DeviceIdType.MESH


def tables():
    sample_index = np.arange(L, dtype=np.int64)[:, None]
    bin_index = np.arange(F, dtype=np.int64)[None, :] + 1
    phase_index = sample_index * bin_index % L
    angle = phase_index.astype(np.float32) * np.float32(2.0 * math.pi / L)
    cosine, sine = np.cos(angle), -np.sin(angle)
    table = np.concatenate(
        [cosine[:, :FULL], sine[:, :FULL], cosine[:, FULL:], sine[:, FULL:]], axis=1
    ).astype(np.float32)
    high = table.astype(ml_dtypes.bfloat16)
    lag_rows = np.concatenate([np.arange(L - HL, L), np.arange(HL)])
    low = (table - high.astype(np.float32)).astype(ml_dtypes.bfloat16)[lag_rows]
    return high, low


def dot(left, right):
    return jnp.dot(left, right, preferred_element_type=jnp.float32)


def dot_rows(left, right):
    return lax.dot_general(left, right, (((1,), (1,)), ((), ())), preferred_element_type=jnp.float32)


def split(value):
    high = value.astype(jnp.bfloat16)
    return high, (value - high.astype(jnp.float32)).astype(jnp.bfloat16)


def band_matrix():
    width = FULL + LANES
    row = lax.broadcasted_iota(jnp.int32, (width, width), 0)
    col = lax.broadcasted_iota(jnp.int32, (width, width), 1)
    out_bin = jnp.where(col < F, col, col - HALF)
    centre = jnp.clip(out_bin, SMOOTH, F - 1 - SMOOTH)
    near = (jnp.abs(row - centre) <= SMOOTH) & (row < F)
    return jnp.where(near, 1.0, 0.0).astype(jnp.bfloat16)


def whiten(signal, table, band):
    mean = jnp.sum(signal, axis=1, keepdims=True) * (1.0 / L)
    spectrum = dot((signal - mean).astype(jnp.bfloat16), table)
    real, imag, mixed = spectrum[:, :FULL], spectrum[:, FULL : 2 * FULL], spectrum[:, 2 * FULL :]
    squares = mixed * mixed
    power = jnp.concatenate([real * real + imag * imag, squares + pltpu.roll(squares, HALF, 1)], axis=1)
    amplitude = jnp.sqrt(power)
    first, rest = split(amplitude)
    second, third = split(amplitude - first.astype(jnp.float32))
    smooth = (dot(first, band) + dot(second, band) + dot(third, band)) / (2 * SMOOTH + 1)
    factor = 1.0 / (smooth + 1e-06)
    return jnp.concatenate(
        [real * factor[:, :FULL], imag * factor[:, :FULL], mixed * factor[:, FULL:]], axis=1
    )


def kernel(
    dims,
    rec_hbm,
    table_hbm,
    low_hbm,
    partners_hbm,
    counts_hbm,
    sources_hbm,
    out_ref,
    partners_ref,
    counts_ref,
    sources_ref,
    rec,
    table,
    lag_high,
    lag_low,
    band,
    white_send,
    white_recv,
    near_send,
    near_recv,
    near_rows,
    far_send,
    far_recv,
    source_full,
    source_rest,
    partner_rows,
    cross,
    stack_send,
    stack_recvs,
    local_sems,
    near_sems,
    far_sems,
    swap_sems,
    white_sems,
    stack_sems,
):
    blocks, shares, pieces, slots, sources = dims
    planes = shares // CORES
    me_chan, me_tm = lax.axis_index("chan"), lax.axis_index("tm")
    me_plane, me_core = lax.div(me_tm, CORES), lax.rem(me_tm, CORES)

    def tm_index(step, core_step):
        return lax.rem(me_plane + step, planes) * CORES + lax.rem(me_core + core_step, CORES)

    steps = sorted(range(1, planes), key=lambda step: -min(step, planes - step))
    near_peers = [("tm", tm_index(step, 0)) for step in steps]
    partner = ("tm", tm_index(0, 1))
    tm_peers = [("tm", tm_index(step, core_step)) for step in steps for core_step in range(CORES)] + [partner]
    chan_peers = [("chan", lax.rem(me_chan + step, blocks)) for step in range(1, blocks)]

    barrier = pltpu.get_barrier_semaphore()
    for axis, peer in tm_peers + chan_peers:
        pl.semaphore_signal(barrier, inc=1, device_id={axis: peer}, device_id_type=MESH)

    index_loads = [
        pltpu.make_async_copy(sources_hbm, sources_ref, local_sems.at[0]),
        pltpu.make_async_copy(partners_hbm, partners_ref, local_sems.at[1]),
        pltpu.make_async_copy(counts_hbm, counts_ref, local_sems.at[2]),
    ]
    loads = [
        pltpu.make_async_copy(rec_hbm.at[:, piece], rec.at[piece], local_sems.at[7 + piece]) for piece in range(pieces)
    ]
    table_load = pltpu.make_async_copy(table_hbm, table, local_sems.at[3])
    lag_loads = [
        pltpu.make_async_copy(table_hbm.at[pl.ds(L - HL, HL)], lag_high.at[pl.ds(0, HL)], local_sems.at[4]),
        pltpu.make_async_copy(table_hbm.at[pl.ds(0, HL)], lag_high.at[pl.ds(HL, HL)], local_sems.at[5]),
        pltpu.make_async_copy(low_hbm, lag_low, local_sems.at[6]),
    ]
    for copy in index_loads + loads + [table_load] + lag_loads:
        copy.start()

    def send(src, dst, sems, peer):
        axis, index = peer
        pltpu.make_async_remote_copy(
            src_ref=src, dst_ref=dst, send_sem=sems[0], recv_sem=sems[1], device_id={axis: index}, device_id_type=MESH
        ).start()

    def wait_bytes(ref, sem):
        pltpu.make_async_copy(ref, ref, sem).wait()

    band[...] = band_matrix()
    for copy in index_loads + loads:
        copy.wait()

    row_id = lax.broadcasted_iota(jnp.int32, (ROWS, L), 0)
    head_id = lax.broadcasted_iota(jnp.int32, (2 * ROWS, L), 0)
    head = jnp.zeros((2 * ROWS, L), jnp.float32)
    for source in range(sources):
        channel = sources_ref[0, source]
        share = lax.div(channel, pieces * ROWS)
        within = channel - share * (pieces * ROWS)
        piece = lax.div(within, ROWS)
        tile = rec[piece, share].astype(jnp.float32)
        row = jnp.sum(jnp.where(row_id == within - piece * ROWS, tile, 0.0), axis=0, keepdims=True)
        head = jnp.where(head_id == source, row, head)
    table_load.wait()
    near_send[...] = whiten(head, table[...], band[...])[:sources].astype(jnp.bfloat16).astype(jnp.float32)
    near_recv[me_plane] = near_send[...]
    pl.semaphore_wait(barrier, len(tm_peers) + len(chan_peers))
    for peer in near_peers:
        send(near_send, near_recv.at[me_plane], (near_sems.at[0], near_sems.at[1]), peer)

    for piece in range(pieces):
        white = whiten(rec[piece].astype(jnp.float32).reshape(shares * ROWS, L), table[...], band[...])
        white_send[piece] = white.reshape(shares, ROWS, COLS).astype(jnp.bfloat16)
        white_recv[piece, me_tm] = white_send[piece, me_tm]
        for peer in tm_peers:
            send(
                white_send.at[piece, peer[1]],
                white_recv.at[piece, me_tm],
                (white_sems.at[0, piece], white_sems.at[1, piece]),
                peer,
            )

    wait_bytes(near_recv.at[pl.ds(0, planes - 1)], near_sems.at[1])
    for plane in range(planes):
        for source in range(sources):
            near_rows[pl.ds(source * planes + plane, 1), :] = near_recv[plane, pl.ds(source, 1), :]
    far_send[...] = near_rows[...].astype(jnp.bfloat16)
    far_recv[me_core, me_chan] = far_send[...]
    for peer in chan_peers:
        send(far_send, far_recv.at[me_core, me_chan], (far_sems.at[0], far_sems.at[1]), peer)
    wait_bytes(far_recv.at[0, pl.ds(0, blocks - 1)], far_sems.at[1])
    send(far_recv.at[me_core], far_recv.at[me_core], (swap_sems.at[0], swap_sems.at[1]), partner)

    tiles = FULL // LANES
    lower = lax.broadcasted_iota(jnp.int32, (1, planes, LANES), 2) < HALF

    def unpack(core):
        rows = far_recv[core].astype(jnp.float32)
        for tile in range(tiles):
            real = rows[:, :, tile * LANES : (tile + 1) * LANES]
            imag = rows[:, :, (tiles + tile) * LANES : (tiles + tile + 1) * LANES]
            source_full[core, :, tile] = real
            source_full[core, :, tiles + tile] = imag
            source_full[core, :, 2 * tiles + tile] = real - imag
        first, second = rows[:, :planes, 2 * FULL :], rows[:, planes:, 2 * FULL :]
        real = jnp.where(lower, first, pltpu.roll(second, HALF, 2))
        imag = jnp.where(lower, pltpu.roll(first, HALF, 2), second)
        source_rest[core, :, 0] = real
        source_rest[core, :, 1] = imag
        source_rest[core, :, 2] = real - imag

    unpack(me_core)
    wait_bytes(far_recv.at[0], swap_sems.at[1])
    unpack(1 - me_core)

    for copy in lag_loads:
        copy.wait()
    lane_low = lax.broadcasted_iota(jnp.int32, (ROWS, LANES), 1) < HALF
    scale = 1.0 / math.sqrt(F * shares)

    def products(reals, imags, sums, a_real, a_imag, a_diff, b_real, b_imag, b_sum):
        return reals + a_real * b_real, imags + a_imag * b_imag, sums + a_diff * b_sum

    for piece in range(pieces):
        wait_bytes(white_recv.at[piece, pl.ds(0, shares - 1)], white_sems.at[1, piece])
        spectra = white_recv[piece].astype(jnp.float32)
        real, imag = spectra[:, :, :FULL], spectra[:, :, FULL : 2 * FULL]
        mixed = spectra[:, :, 2 * FULL :]
        turned = pltpu.roll(mixed, HALF, 2)
        rest_low = lax.broadcasted_iota(jnp.int32, mixed.shape, 2) < HALF
        rest_real, rest_imag = jnp.where(rest_low, mixed, turned), jnp.where(rest_low, turned, mixed)
        partner_rows[:, :, : 2 * FULL] = spectra[:, :, : 2 * FULL]
        partner_rows[:, :, 2 * FULL : 3 * FULL] = real + imag
        for index, value in enumerate((rest_real, rest_imag, rest_real + rest_imag)):
            partner_rows[:, :, 3 * FULL + index * LANES : 3 * FULL + (index + 1) * LANES] = value

        def some_blocks(group, carry):
            members = [group * TOGETHER + member for member in range(TOGETHER)]

            def partner_tile(window, tile):
                return partner_rows[window, :, pl.ds(tile * LANES, LANES)]

            for tile in range(tiles):
                totals = {(m, s): (0.0, 0.0, 0.0) for m in range(TOGETHER) for s in range(sources)}
                for window in range(shares):
                    plane, core = window // CORES, window % CORES
                    b_tiles = [partner_tile(window, kind * tiles + tile) for kind in range(3)]
                    for m, s in totals:
                        a_tiles = [
                            source_full[
                                core, members[m], kind * tiles + tile, pl.ds(s * planes + plane, ROWS, stride=0), :
                            ]
                            for kind in range(3)
                        ]
                        totals[m, s] = products(*totals[m, s], *a_tiles, *b_tiles)
                for (m, s), (reals, imags, sums) in totals.items():
                    row = members[m] * sources + s
                    cross[row, :, pl.ds(tile * LANES, LANES)] = reals + imags
                    cross[row, :, pl.ds((tiles + tile) * LANES, LANES)] = sums - reals + imags
            rest = [(0.0, 0.0, 0.0)] * TOGETHER
            for window in range(shares):
                plane, core = window // CORES, window % CORES
                b_tiles = [partner_tile(window, 3 * tiles + kind) for kind in range(3)]
                for m in range(TOGETHER):
                    a_tiles = [source_rest[core, members[m], kind, pl.ds(plane, ROWS, stride=0), :] for kind in range(3)]
                    rest[m] = products(*rest[m], *a_tiles, *b_tiles)
            for m, (reals, imags, sums) in enumerate(rest):
                real_part, imag_part = reals + imags, sums - reals + imags
                columns = pl.ds(2 * FULL, LANES)
                cross[members[m] * sources, :, columns] = jnp.where(
                    lane_low, real_part, pltpu.roll(imag_part, HALF, 1)
                )
                cross[members[m] * sources + 1, :, columns] = jnp.where(
                    lane_low, pltpu.roll(real_part, HALF, 1), imag_part
                )
            return carry

        lax.fori_loop(0, blocks // TOGETHER, some_blocks, 0)
        high, low = split(cross[...].reshape(blocks * sources * ROWS, COLS))
        lagged = dot_rows(high, lag_high[...]) + dot_rows(low, lag_high[...]) + dot_rows(high, lag_low[...])
        stack_send[piece] = (lagged * scale).reshape(blocks, sources, ROWS, 2 * HL).astype(jnp.bfloat16)
        stack_recvs[piece][me_chan] = stack_send[piece, me_chan]
        for peer in chan_peers:
            send(
                stack_send.at[piece, peer[1]],
                stack_recvs[piece].at[me_chan],
                (stack_sems.at[0, piece], stack_sems.at[1, piece]),
                peer,
            )

    for piece in range(pieces):
        wait_bytes(stack_recvs[piece].at[pl.ds(0, blocks - 1)], stack_sems.at[1, piece])
        for slot in range(slots):
            stack = stack_recvs[piece][partners_ref[0, slot]].astype(jnp.float32)
            out_ref[slot, :, pl.ds(piece * ROWS, ROWS), :] = jnp.where(slot < counts_ref[0], stack, 0.0)

    wait_bytes(near_recv.at[pl.ds(0, planes - 1)], near_sems.at[0])
    wait_bytes(far_recv.at[0, pl.ds(0, blocks - 1)], far_sems.at[0])
    wait_bytes(far_recv.at[0], swap_sems.at[0])
    for piece in range(pieces):
        wait_bytes(white_recv.at[piece, pl.ds(0, shares - 1)], white_sems.at[0, piece])
        wait_bytes(stack_recvs[piece].at[pl.ds(0, blocks - 1)], stack_sems.at[0, piece])


def local(blocks, shares, records, partners, counts, sources):
    channels = records.shape[1]
    slots, picks = partners.shape[1], sources.shape[1]
    pieces = channels // (shares * ROWS)
    high, low = tables()
    bf16, f32 = jnp.bfloat16, jnp.float32
    planes, tiles = shares // CORES, FULL // LANES
    result = pl.pallas_call(
        functools.partial(kernel, (blocks, shares, pieces, slots, picks)),
        out_shape=jax.ShapeDtypeStruct((slots, picks, pieces * ROWS, 2 * HL), f32),
        in_specs=[pl.BlockSpec(memory_space=pl.ANY)] * 6,
        out_specs=pl.BlockSpec(memory_space=pltpu.VMEM),
        scratch_shapes=[
            pltpu.SMEM((1, slots), jnp.int32),
            pltpu.SMEM((1,), jnp.int32),
            pltpu.SMEM((1, picks), jnp.int32),
            pltpu.VMEM((pieces, shares, ROWS, L), bf16),
            pltpu.VMEM((L, COLS), bf16),
            pltpu.VMEM((2 * HL, COLS), bf16),
            pltpu.VMEM((2 * HL, COLS), bf16),
            pltpu.VMEM((FULL + LANES, FULL + LANES), bf16),
            pltpu.VMEM((pieces, shares, ROWS, COLS), bf16),
            pltpu.VMEM((pieces, shares, ROWS, COLS), bf16),
            pltpu.VMEM((picks, COLS), f32),
            pltpu.VMEM((planes, picks, COLS), f32),
            pltpu.VMEM((planes * picks, COLS), f32),
            pltpu.VMEM((planes * picks, COLS), bf16),
            pltpu.VMEM((CORES, blocks, planes * picks, COLS), bf16),
            pltpu.VMEM((CORES, blocks, 3 * tiles, planes * picks, LANES), f32),
            pltpu.VMEM((CORES, blocks, 3, planes, LANES), f32),
            pltpu.VMEM((shares, ROWS, 3 * FULL + 3 * LANES), f32),
            pltpu.VMEM((blocks * picks, ROWS, COLS), f32),
            pltpu.VMEM((pieces, blocks, picks, ROWS, 2 * HL), bf16),
            [pltpu.VMEM((blocks, picks, ROWS, 2 * HL), bf16) for _ in range(pieces)],
            pltpu.SemaphoreType.DMA((7 + pieces,)),
            pltpu.SemaphoreType.DMA((2,)),
            pltpu.SemaphoreType.DMA((2,)),
            pltpu.SemaphoreType.DMA((2,)),
            pltpu.SemaphoreType.DMA((2, pieces)),
            pltpu.SemaphoreType.DMA((2, pieces)),
        ],
        compiler_params=pltpu.CompilerParams(
            collective_id=0, has_side_effects=True, vmem_limit_bytes=67_043_328
        ),
        name="correlate",
    )(
        records.reshape(shares, pieces, ROWS, L),
        jnp.asarray(high),
        jnp.asarray(low),
        partners,
        counts,
        sources,
    )
    return result.transpose(2, 0, 1, 3)[None]


def solution(mesh):
    return jax.shard_map(
        functools.partial(local, mesh.shape["chan"], mesh.shape["tm"]),
        mesh=mesh,
        in_specs=(P("tm", "chan", None), P("chan", None), P("chan"), P("chan", None)),
        out_specs=P("chan", "tm", None, None, None),
        check_vma=False,
    )
```

time: 48.3 us -> 39.1 us (0.81)
  Pallas kernels: 41.3 us -> 36.6 us
  local copies, waits for them, and re-layouts: 5.95 us -> 1.74 us
    unnamed x10 -> x0, local copies, waits for them, and re-layouts: 5.15 us -> none
    pallas_call x1, Pallas kernels: 41.3 us -> 36.6 us  [local(): pl.pallas_call(functools.partial(kernel, (blocks, shares, pieces, slots,...]
    broadcast_in_dim x1, local copies, waits for them, and re-layouts: 0.8 us -> 1.74 us  [local(): return result.transpose(2, 0, 1, 3)[None]]
where the time goes in v2:
time: 39.1 us; the launch traced here: 39 us
  Pallas kernels  36.6 us (94%)
  local copies, waits for them, and re-layouts  1.74 us (4%)
  between operations  0.66 us (2%)
    pallas_call x1, Pallas kernels, local(): pl.pallas_call(functools.partial(kernel, (blocks, shares, pieces, slots,...  36.6 us
    broadcast_in_dim x1, local copies, waits for them, and re-layouts, local(): return result.transpose(2, 0, 1, 3)[None]  1.74 us

profile of v2, /device:TPU:1, one launch (start us, length us, event | category | flops | bytes accessed | tf_op | source)
XLA Modules:
  0.0 39.0 jit_solution(7024853173045358558)
XLA Ops:
  0.7 36.6 %correlate.1 = f32[3,2,24,384]{3,2,1,0:T(8,128)} custom-call(bf16[16,3,8,1536]{3,2,1,0:T(8,128)(2,1)} %bitcast.4, bf16[1536,640]{1,0:T(8,128)(2,1)} %constant.4.clone.table_hbm, bf16[384,640]{1,0:T(8,128)(2,1)} %constant.5.clone.low_hbm, s32[1,3]{1,0:T(1,128)} %partners_hbm.1, s32[1]{0:T(128)S(6)} %copy.8.counts_hbm, s32[1,2]{1,0:T(1,128)} %sources_hbm.1), custom_call_target="tpu_custom_call" | custom-call | tf_op jit(solution)/shard_map/correlate/pallas_call | solution.py:325
  37.2 1.7 %copy.7 = f32[1,24,3,2,384]{4,3,2,1,0:T(2,128)} copy(f32[1,24,3,2,384]{4,1,3,2,0:T(8,128)} %bitcast.5) | data formatting | bytes 442368 | tf_op jit(solution)/shard_map/broadcast_in_dim | solution.py:371
